TPU v7x, 32 devices: a whole 2x2x4 slice. The times are simulated.
32 devices in a mesh: group: 2 (over y), clip: 4 (over x, core), seq: 4 (over z).
Axes of the slice: x: 2, y: 2, z: 4, core: 2. Of those that a mesh axis runs over, the one named last changes fastest.
Arguments:
- queries: bfloat16 [8, 512, 2048], P(('group', 'clip'), 'seq'), parts along dimension 0, may hold values from -18 to 18
- key_states: bfloat16 [8, 512, 2048], P(('group', 'clip'), 'seq'), parts along dimension 0, may hold values from -18 to 18
- value_states: bfloat16 [8, 512, 2048], P(('group', 'clip'), 'seq'), parts along dimension 0, may hold values from -6 to 6
- query_tangent: bfloat16 [8, 512, 2048], P(('group', 'clip'), 'seq'), parts along dimension 0, may hold values from -6 to 6
- key_tangent: bfloat16 [8, 512, 2048], P(('group', 'clip'), 'seq'), parts along dimension 0, may hold values from -6 to 6
- value_tangent: bfloat16 [8, 512, 2048], P(('group', 'clip'), 'seq'), parts along dimension 0, may hold values from -6 to 6
- offsets: int32 [8], P(('group', 'clip')), parts along dimension 0, may hold values from 0 to 130560
Outputs:
- attended: bfloat16 [8, 512, 2048], P(('group', 'clip'), 'seq'), parts along dimension 0
- attended_tangent: bfloat16 [8, 512, 2048], P(('group', 'clip'), 'seq'), parts along dimension 0
There are 2 independent parts, one for each index of `group`. A program takes and returns all parts, laid end to end along the dimension named above; each array names one. Nothing has to cross between parts.
All inputs are finite; a program needn't handle non-finite values.
Results may differ from a plain program's by a relative error of at most 0.012.
The roundings to bfloat16 on the way count: a program that leaves them out, or rounds other values in their place, can miss the bound.
Values may be sent and summed in bfloat16 or wider, within the bound.
No kernel may reach another device: no remote copies, remote signals or barrier semaphores. Data moves between devices by JAX's collectives and lax.ppermute only.
A program may use at most 64 MiB of HBM per device.

v0:
```python
import math
import jax
import jax.numpy as jnp
from jax import lax
from jax.sharding import PartitionSpec as P

H = 16
HD = 128
HH = 44
WW = 80
rope_theta = 10000.0


def rope_tables(first, count):
    global_index = first + jnp.arange(count, dtype=jnp.int32)
    frames = global_index // (HH * WW)
    grid_row = global_index // WW % HH
    column = global_index % WW
    spatial = HD // 6 * 2
    temporal = HD - 2 * spatial
    channel = jnp.arange(HD, dtype=jnp.int32)
    part_start = jnp.where(
        channel < temporal, 0, jnp.where(channel < temporal + spatial, temporal, temporal + spatial)
    )
    extent = jnp.where(channel < temporal, temporal, spatial)
    pair_index = (channel - part_start) // 2
    frequency = jnp.exp(
        -(2.0 * pair_index.astype(jnp.float32) / extent.astype(jnp.float32)) * math.log(rope_theta)
    )
    position = jnp.where(
        channel[None, :] < temporal,
        frames[:, None],
        jnp.where(channel[None, :] < temporal + spatial, grid_row[:, None], column[:, None]),
    )
    angles = position.astype(jnp.float32) * frequency[None, :]
    return (jnp.cos(angles)[:, None, :], jnp.sin(angles)[:, None, :])


def rotate(tensor, cosine, sine):
    channel = jnp.arange(tensor.shape[-1], dtype=jnp.int32)
    partner = jnp.where(
        channel % 2 == 0, -jnp.roll(tensor, -1, axis=-1), jnp.roll(tensor, 1, axis=-1)
    )
    return (tensor * cosine + partner * sine).astype(jnp.bfloat16)


def primal_terms(query_blk, keys_all, values_all, scaling):
    scores = (
        jnp.einsum("bhd,khd->hbk", query_blk, keys_all, preferred_element_type=jnp.float32)
        * scaling
    )
    largest = jnp.max(scores, axis=-1, keepdims=True)
    expons = jnp.exp(scores - largest)
    probs = expons / jnp.sum(expons, axis=-1, keepdims=True)
    weights = probs.astype(jnp.bfloat16)
    out_full = jnp.einsum("hbk,khd->bhd", weights, values_all, preferred_element_type=jnp.float32)
    return (weights, out_full)


def tangent_terms(
    query_blk, qdot_blk, keys_all, kdots_all, values_all, vdots_all, weights, out_full, scaling
):
    scores_dot = (
        jnp.einsum("bhd,khd->hbk", qdot_blk, keys_all, preferred_element_type=jnp.float32)
        + jnp.einsum("bhd,khd->hbk", query_blk, kdots_all, preferred_element_type=jnp.float32)
    ) * scaling
    product = weights.astype(jnp.float32) * scores_dot
    correction = jnp.sum(product, axis=-1)
    product_half = product.astype(jnp.bfloat16)
    tangent = (
        jnp.einsum("hbk,khd->bhd", weights, vdots_all, preferred_element_type=jnp.float32)
        + jnp.einsum("hbk,khd->bhd", product_half, values_all, preferred_element_type=jnp.float32)
        - jnp.transpose(correction)[:, :, None] * out_full
    )
    return tangent.astype(jnp.bfloat16)


def body(queries, key_states, value_states, query_tangent, key_tangent, value_tangent, offsets):
    devices = lax.axis_size("seq")
    repeat = max(devices // H, 1)
    per_device = max(H // devices, 1)
    groups = H // per_device
    width = per_device * HD
    tokens = queries.shape[1]
    sub_rows = tokens // repeat
    scaling = 1.0 / math.sqrt(HD)
    first = offsets[0] + lax.axis_index("seq") * tokens
    cosine, sine = rope_tables(first, tokens)

    def roped(array):
        return rotate(array[0].reshape(tokens, H, HD).astype(jnp.float32), cosine, sine).reshape(
            tokens, H * HD
        )

    def by_rows(array):
        shaped = array.reshape(repeat, sub_rows, groups, width)
        return jnp.transpose(shaped, (2, 0, 1, 3)).reshape(devices, sub_rows, width)

    def by_copies(array):
        shaped = jnp.transpose(array.reshape(tokens, groups, width), (1, 0, 2))
        spread = jnp.broadcast_to(shaped[:, None], (groups, repeat, tokens, width))
        return spread.reshape(devices, tokens, width)

    query_send = by_rows(roped(queries))
    qdot_send = by_rows(roped(query_tangent))
    key_send = by_copies(roped(key_states))
    kdot_send = by_copies(roped(key_tangent))
    value_send = by_copies(value_states[0])
    vdot_send = by_copies(value_tangent[0])
    query_rows = devices * sub_rows
    block = min(512, query_rows)
    count = query_rows // block

    def heads_view(array):
        return array.reshape(array.shape[0], per_device, HD)

    def blocks(array):
        return array.reshape(count, block, per_device, HD)

    received = (
        lax.all_to_all(query_send, "seq", split_axis=0, concat_axis=1, tiled=True),
        lax.all_to_all(key_send, "seq", split_axis=0, concat_axis=1, tiled=True),
        lax.all_to_all(value_send, "seq", split_axis=0, concat_axis=1, tiled=True),
        lax.all_to_all(qdot_send, "seq", split_axis=0, concat_axis=1, tiled=True),
        lax.all_to_all(kdot_send, "seq", split_axis=0, concat_axis=1, tiled=True),
        lax.all_to_all(vdot_send, "seq", split_axis=0, concat_axis=1, tiled=True),
    )
    query_in, key_in, value_in, qdot_in, kdot_in, vdot_in = tuple((array[0] for array in received))
    keys_all, values_all = (heads_view(key_in), heads_view(value_in))
    kdots_all, vdots_all = (heads_view(kdot_in), heads_view(vdot_in))

    def one_block(parts):
        query_blk, qdot_blk = parts
        weights, out_full = primal_terms(query_blk, keys_all, values_all, scaling)
        tangent = tangent_terms(
            query_blk,
            qdot_blk,
            keys_all,
            kdots_all,
            values_all,
            vdots_all,
            weights,
            out_full,
            scaling,
        )
        return (out_full.astype(jnp.bfloat16), tangent)

    attended, tangent_out = lax.map(one_block, (blocks(query_in), blocks(qdot_in)))

    def to_sources(array):
        return array.reshape(devices, sub_rows, width)

    returned = (
        lax.all_to_all(to_sources(attended), "seq", split_axis=0, concat_axis=0, tiled=True),
        lax.all_to_all(to_sources(tangent_out), "seq", split_axis=0, concat_axis=0, tiled=True),
    )

    def to_tokens(array):
        shaped = array.reshape(groups, repeat, sub_rows, width)
        return jnp.transpose(shaped, (1, 2, 0, 3)).reshape(tokens, H * HD)[None]

    return (to_tokens(returned[0]), to_tokens(returned[1]))


def solution(mesh):
    in_specs = (
        P(("group", "clip"), "seq", None),
        P(("group", "clip"), "seq", None),
        P(("group", "clip"), "seq", None),
        P(("group", "clip"), "seq", None),
        P(("group", "clip"), "seq", None),
        P(("group", "clip"), "seq", None),
        P(("group", "clip")),
    )
    out_specs = (P(("group", "clip"), "seq", None), P(("group", "clip"), "seq", None))
    return jax.shard_map(body, mesh=mesh, in_specs=in_specs, out_specs=out_specs, check_vma=False)
```

profile of v0, /device:TPU:0, one launch (start us, length us, event | category | flops | bytes accessed | tf_op | source)
XLA Modules:
  0.0 167.7 jit_solution(8478201329883006545)
XLA Ops:
  0.6 1.3 copy.48
  1.9 1.5 fusion.48
  3.5 0.2 copy.32
  3.7 1.2 fusion.50
  5.7 1.9 %maximum_negate_fusion.2 = (f32[128,16,128]{0,2,1:T(8,128)S(1)}, f32[128,16,128]{0,2,1:T(8,128)S(1)}) fusion(f32[128,16,1]{0,2,1:T(1,128)S(1)} %get-tuple-element.40, f32[128,16,127]{0,2,1:T(8,128)} %get-tuple-element.42, f32[128,16,127]{0,2,1:T(8,128)} %get-tuple-element.41, f32[128,16,1]{0,2,1:T(1,128)S(1)} %get-tuple-element.39), kind=kLoop, calls=%fused_computation.26 | loop fusion | flops 786432 | bytes 4194304 | tf_op jit(solution)/shard_map/neg | solution.py:42
  7.6 0.2 maximum_negate_fusion
  7.8 0.3 fusion.40
  8.1 0.1 mul.161
  8.3 0.1 mul.164
  8.4 1.8 %fusion.24 = (bf16[4,128,512]{1,2,0:T(8,128)(2,1)}, bf16[4,128,512]{1,2,0:T(8,128)(2,1)}) fusion(f32[1,128,4,512]{1,3,2,0:T(8,128)S(1)} %bitcast.120, f32[1,128,4,512]{1,3,2,0:T(8,128)S(1)} %bitcast.122, f32[1,128,4,512]{1,3,2,0:T(8,128)S(1)} %bitcast.123, f32[1,128,4,512]{1,3,2,0:T(8,128)S(1)} %bitcast.108, f32[1,128,4,512]{1,3,2,0:T(8,128)S(1)} %bitcast.118, ...), kind=kLoop, calls=%fused_computation.35 | loop fusion | flops 2621440 | bytes 9437696 | tf_op jit(solution)/shard_map/reshape | solution.py:97
  10.1 6.3 %all-to-all-start = ((bf16[4,128,512]{1,2,0:T(8,128)(2,1)}), bf16[4,128,512]{1,2,0:T(8,128)(2,1)}, u32[]{:S(2)}, u32[]{:S(2)}) async-start(bf16[4,128,512]{1,2,0:T(8,128)(2,1)} %get-tuple-element.25), calls=%async_computation | async-start | bytes 1048576 | tf_op jit(solution)/shard_map/all_to_all | solution.py:121
  16.5 1.2 copy.35
  17.7 1.5 fusion.51
  19.2 1.2 copy.53
  20.5 0.2 fusion.45
  20.7 1.0 copy-done.6
  21.7 0.3 copy-done.7
  22.0 0.3 maximum_negate_fusion.1
  22.3 0.3 maximum_negate_fusion.3
  22.6 0.6 copy-done.1
  23.2 1.7 %fusion.25 = (bf16[4,128,512]{1,2,0:T(8,128)(2,1)}, bf16[4,128,512]{1,2,0:T(8,128)(2,1)}) fusion(f32[128,4,512]{0,2,1:T(8,128)S(1)} %bitcast.117, pred[512]{0:T(512)(128)(4,1)S(1)} %broadcast_bitcast_fusion, f32[128,4,512]{0,2,1:T(8,128)S(1)} %bitcast.114, f32[128,4,512]{0,2,1:T(8,128)S(1)} %bitcast.121, f32[128,4,512]{0,2,1:T(8,128)S(1)} %bitcast.129, ...), kind=kLoop, calls=%fused_computation.36 | loop fusion | flops 2621440 | bytes 9437696 | tf_op jit(solution)/shard_map/transpose | solution.py:100
  25.0 6.1 %all-to-all-done = bf16[4,128,512]{1,2,0:T(8,128)(2,1)} async-done(((bf16[4,128,512]{1,2,0:T(8,128)(2,1)}), bf16[4,128,512]{1,2,0:T(8,128)(2,1)}, u32[]{:S(2)}, u32[]{:S(2)}) %all-to-all-start) | async-done | bytes 524320 | tf_op jit(solution)/shard_map/all_to_all | solution.py:121
  31.1 17.5 %all_to_all.64 = bf16[4,128,512]{1,2,0:T(8,128)(2,1)S(1)} all-to-all(bf16[4,128,512]{1,2,0:T(8,128)(2,1)} %get-tuple-element.23), channel_id=1, replica_groups=mesh['group'=2,'clip'=4,'seq'=4] {'seq'}, dimensions={0} | all-to-all | bytes 1048576 | tf_op jit(solution)/shard_map/all_to_all | solution.py:122
  48.6 17.7 %all_to_all.65 = bf16[4,128,512]{1,2,0:T(8,128)(2,1)} all-to-all(bf16[4,128,512]{1,2,0:T(8,128)(2,1)} %get-tuple-element.24), channel_id=1, replica_groups=mesh['group'=2,'clip'=4,'seq'=4] {'seq'}, dimensions={0} | all-to-all | bytes 1048576 | tf_op jit(solution)/shard_map/all_to_all | solution.py:124
  66.3 3.5 %all-to-all-start.6 = ((bf16[4,128,512]{1,2,0:T(8,128)(2,1)}), bf16[4,128,512]{1,2,0:T(8,128)(2,1)S(1)}, u32[]{:S(2)}, u32[]{:S(2)}) async-start(bf16[4,128,512]{1,2,0:T(8,128)(2,1)} %get-tuple-element.22), calls=%async_computation.6 | async-start | bytes 1048576 | tf_op jit(solution)/shard_map/all_to_all | solution.py:125
  69.7 1.4 reshape_squeeze.25
  71.2 0.9 copy.94
  72.1 0.4 reshape_squeeze.27
  72.4 0.9 copy.93
  73.3 1.2 copy.34
  74.6 0.1 squeeze.13
  74.7 0.2 copy.37
  74.9 0.1 reshape_squeeze.24
  75.1 8.2 %all-to-all-done.6 = bf16[4,128,512]{1,2,0:T(8,128)(2,1)S(1)} async-done(((bf16[4,128,512]{1,2,0:T(8,128)(2,1)}), bf16[4,128,512]{1,2,0:T(8,128)(2,1)S(1)}, u32[]{:S(2)}, u32[]{:S(2)}) %all-to-all-start.6) | async-done | bytes 524320 | tf_op jit(solution)/shard_map/all_to_all | solution.py:125
  83.3 3.5 %all-to-all-start.2 = ((bf16[4,128,512]{2,1,0:T(8,128)(2,1)}), bf16[4,128,512]{2,1,0:T(8,128)(2,1)S(1)}, u32[]{:S(2)}, u32[]{:S(2)}) async-start(bf16[4,128,512]{2,1,0:T(8,128)(2,1)} %bitcast.100), calls=%async_computation.2 | async-start | bytes 1048576 | tf_op jit(solution)/shard_map/all_to_all | solution.py:123
  86.8 0.7 fusion.35
  87.5 3.1 %fusion.53 = (f32[4,512]{1,0:T(4,128)S(1)}, f32[4,512,512]{1,2,0:T(8,128)}) fusion(f32[4,512,512]{1,2,0:T(8,128)S(1)} %fusion.35), kind=kOutput, calls=%fused_computation.82 | output fusion | flops 4194815 | bytes 8396800 | tf_op jit(solution)/shard_map/while/body/eval_jaxpr/sub | solution.py:53
  90.6 10.2 %all-to-all-done.2 = bf16[4,128,512]{2,1,0:T(8,128)(2,1)S(1)} async-done(((bf16[4,128,512]{2,1,0:T(8,128)(2,1)}), bf16[4,128,512]{2,1,0:T(8,128)(2,1)S(1)}, u32[]{:S(2)}, u32[]{:S(2)}) %all-to-all-start.2) | async-done | bytes 524320 | tf_op jit(solution)/shard_map/all_to_all | solution.py:123
  100.8 4.3 %all-to-all-start.4 = ((bf16[4,128,512]{2,1,0:T(8,128)(2,1)}), bf16[4,128,512]{2,1,0:T(8,128)(2,1)}, u32[]{:S(2)}, u32[]{:S(2)}) async-start(bf16[4,128,512]{2,1,0:T(8,128)(2,1)} %bitcast.99), calls=%async_computation.4 | async-start | bytes 1048576 | tf_op jit(solution)/shard_map/all_to_all | solution.py:126
  105.1 2.8 %divide_convert_fusion = bf16[4,512,512]{1,2,0:T(8,128)(2,1)S(1)} fusion(f32[4,512,512]{1,2,0:T(8,128)} %get-tuple-element.54, f32[4,512]{1,0:T(4,128)S(1)} %get-tuple-element.53), kind=kLoop, calls=%fused_computation.2 | loop fusion | flops 2097152 | bytes 6299648 | tf_op jit(solution)/shard_map/while/body/eval_jaxpr/convert_element_type | solution.py:55
  107.9 2.0 %copy.50 = bf16[4,128,512]{2,1,0:T(8,128)(2,1)} copy(bf16[4,128,512]{1,2,0:T(8,128)(2,1)} %all_to_all.65) | data formatting | bytes 1048576 | tf_op jit(solution)/shard_map/all_to_all | solution.py:124
  109.9 2.0 %squeeze.14 = bf16[512,4,128]{2,1,0:T(4,128)(2,1)} reshape(bf16[4,128,512]{2,1,0:T(8,128)(2,1)} %copy.50) | data formatting | bytes 1048576 | tf_op jit(solution)/shard_map/while/body/jit(dynamic_index_in_dim)/squeeze | solution.py:148
  111.9 1.0 copy.55
  112.9 1.9 %reshape_squeeze.29 = bf16[512,4,128]{2,1,0:T(4,128)(2,1)} reshape(bf16[4,128,512]{2,1,0:T(8,128)(2,1)} %copy.55) | data formatting | bytes 1048576 | tf_op jit(solution)/shard_map/reshape;squeeze | solution.py:115
  114.9 1.2 reshape_squeeze.26
  116.0 2.0 %fusion.54 = (bf16[512,4,128]{2,0,1:T(8,128)(2,1)}, f32[512,4,128]{2,0,1:T(8,128)}) fusion(bf16[4,512,512]{1,2,0:T(8,128)(2,1)S(1)} %divide_convert_fusion, bf16[512,4,128]{2,1,0:T(4,128)(2,1)S(1)} %reshape_squeeze.26), kind=kOutput, calls=%fused_computation.83 | convolution fusion | flops 268697600 | bytes 4194304 | tf_op jit(solution)/shard_map/while/body/eval_jaxpr/hbk,khd->bhd/dot_general | solution.py:56
  118.1 2.7 %fusion.28 = f32[4,512,512]{1,2,0:T(8,128)} fusion(bf16[512,4,128]{2,1,0:T(4,128)(2,1)S(1)} %copy-done.8, bf16[512,4,128]{2,1,0:T(4,128)(2,1)S(1)} %reshape_squeeze.24), kind=kOutput, calls=%fused_computation.39 | convolution fusion | flops 268435456 | bytes 5242880 | tf_op jit(solution)/shard_map/while/body/eval_jaxpr/bhd,khd->hbk/dot_general | solution.py:64
  120.8 2.0 %reshape_squeeze.28 = bf16[512,4,128]{2,1,0:T(4,128)(2,1)} reshape(bf16[4,128,512]{2,1,0:T(8,128)(2,1)} %all-to-all-done.4) | data formatting | bytes 1048576 | tf_op jit(solution)/shard_map/reshape;squeeze | solution.py:115
  122.8 1.9 %fusion.30 = f32[4,512,128]{2,1,0:T(8,128)S(1)} fusion(bf16[4,512,512]{1,2,0:T(8,128)(2,1)S(1)} %divide_convert_fusion, bf16[512,4,128]{2,1,0:T(4,128)(2,1)} %reshape_squeeze.28), kind=kOutput, calls=%fused_computation.41 | convolution fusion | flops 268435456 | bytes 3670016 | tf_op jit(solution)/shard_map/while/body/eval_jaxpr/hbk,khd->bhd/dot_general | solution.py:71
  124.7 3.5 %fusion.55 = (f32[4,512]{1,0:T(4,128)S(1)}, bf16[4,512,512]{1,2,0:T(8,128)(2,1)S(1)}) fusion(f32[4,512,512]{1,2,0:T(8,128)} %fusion.28, bf16[512,4,128]{2,1,0:T(4,128)(2,1)} %reshape_squeeze.29, bf16[512,4,128]{2,1,0:T(4,128)(2,1)S(1)} %copy-done.3, bf16[4,512,512]{1,2,0:T(8,128)(2,1)S(1)} %divide_convert_fusion), kind=kOutput, calls=%fused_computation.84 | convolution fusion | flops 274724864 | bytes 9445376 | tf_op jit(solution)/shard_map/while/body/eval_jaxpr/bhd,khd->hbk/dot_general | solution.py:65
  128.2 0.0 copy-start.10
  128.2 0.9 fusion.16
  129.1 0.4 copy.60
  129.5 1.0 reshape.425
  130.5 4.9 %all-to-all-start.7 = ((bf16[4,128,512]{2,1,0:T(8,128)(2,1)}), bf16[4,128,512]{2,1,0:T(8,128)(2,1)S(1)}, u32[]{:S(2)}, u32[]{:S(2)}) async-start(bf16[4,128,512]{2,1,0:T(8,128)(2,1)} %reshape.425), calls=%async_computation.7 | async-start | bytes 1048576 | tf_op jit(solution)/shard_map/all_to_all | solution.py:155
  135.4 0.4 copy.43
  135.8 1.0 reshape.422
  136.8 12.1 %all-to-all-done.7 = bf16[4,128,512]{2,1,0:T(8,128)(2,1)S(1)} async-done(((bf16[4,128,512]{2,1,0:T(8,128)(2,1)}), bf16[4,128,512]{2,1,0:T(8,128)(2,1)S(1)}, u32[]{:S(2)}, u32[]{:S(2)}) %all-to-all-start.7) | async-done | bytes 524320 | tf_op jit(solution)/shard_map/all_to_all | solution.py:155
  148.9 3.5 %all-to-all-start.3 = ((bf16[4,128,512]{2,1,0:T(8,128)(2,1)}), bf16[4,128,512]{2,1,0:T(8,128)(2,1)S(1)}, u32[]{:S(2)}, u32[]{:S(2)}) async-start(bf16[4,128,512]{2,1,0:T(8,128)(2,1)} %reshape.422), calls=%async_computation.3 | async-start | bytes 1048576 | tf_op jit(solution)/shard_map/all_to_all | solution.py:154
  152.4 0.3 copy.61
  152.6 1.0 copy.63
  153.7 12.7 %all-to-all-done.3 = bf16[4,128,512]{2,1,0:T(8,128)(2,1)S(1)} async-done(((bf16[4,128,512]{2,1,0:T(8,128)(2,1)}), bf16[4,128,512]{2,1,0:T(8,128)(2,1)S(1)}, u32[]{:S(2)}, u32[]{:S(2)}) %all-to-all-start.3) | async-done | bytes 524320 | tf_op jit(solution)/shard_map/all_to_all | solution.py:154
  166.4 0.3 copy.44
  166.6 1.0 copy.62
  (33 shorter events, 0.2 us)
Async XLA Ops:
  0.6 2.8 %copy-start.11 = (bf16[1,128,2048]{2,1,0:T(8,128)(2,1)S(1)}, bf16[1,128,2048]{2,1,0:T(8,128)(2,1)}, u32[]{:S(2)}) copy-start(bf16[1,128,2048]{2,1,0:T(8,128)(2,1)} %param.7) | copy-start | bytes 1572868
  5.6 2.0 %copy-start.5 = (f32[128,16,127]{0,2,1:T(8,128)S(1)}, f32[128,16,127]{0,2,1:T(8,128)}, u32[]{:S(2)}) copy-start(f32[128,16,127]{0,2,1:T(8,128)} %get-tuple-element.46) | copy-start | bytes 3121156
  8.4 1.8 %copy-start = (f32[128,16,128]{0,2,1:T(8,128)}, f32[128,16,128]{0,2,1:T(8,128)S(1)}, u32[]{:S(2)}) copy-start(f32[128,16,128]{0,2,1:T(8,128)S(1)} %mul.164) | copy-start | bytes 3145732
  10.1 20.9 %all-to-all-start = ((bf16[4,128,512]{1,2,0:T(8,128)(2,1)}), bf16[4,128,512]{1,2,0:T(8,128)(2,1)}, u32[]{:S(2)}, u32[]{:S(2)}) async-start(bf16[4,128,512]{1,2,0:T(8,128)(2,1)} %get-tuple-element.25), calls=%async_computation | async-start | bytes 1048576 | tf_op jit(solution)/shard_map/all_to_all | solution.py:121
  20.4 1.2 copy-start.6
  20.5 1.5 copy-start.7
  22.0 1.2 copy-start.1
  25.0 47.1 %copy-start.12 = (bf16[1,128,2048]{2,1,0:T(8,128)(2,1)S(1)}, bf16[1,128,2048]{2,1,0:T(8,128)(2,1)}, u32[]{:S(2)}) copy-start(bf16[1,128,2048]{2,1,0:T(8,128)(2,1)} %param.12) | copy-start | bytes 1572868
  66.3 17.0 %all-to-all-start.6 = ((bf16[4,128,512]{1,2,0:T(8,128)(2,1)}), bf16[4,128,512]{1,2,0:T(8,128)(2,1)S(1)}, u32[]{:S(2)}, u32[]{:S(2)}) async-start(bf16[4,128,512]{1,2,0:T(8,128)(2,1)} %get-tuple-element.22), calls=%async_computation.6 | async-start | bytes 1048576 | tf_op jit(solution)/shard_map/all_to_all | solution.py:125
  74.7 12.8 %copy-start.2 = (bf16[512,4,128]{2,1,0:T(4,128)(2,1)}, bf16[512,4,128]{2,1,0:T(4,128)(2,1)S(1)}, u32[]{:S(2)}) copy-start(bf16[512,4,128]{2,1,0:T(4,128)(2,1)S(1)} %squeeze.13) | copy-start | bytes 1572868
  83.3 17.5 %all-to-all-start.2 = ((bf16[4,128,512]{2,1,0:T(8,128)(2,1)}), bf16[4,128,512]{2,1,0:T(8,128)(2,1)S(1)}, u32[]{:S(2)}, u32[]{:S(2)}) async-start(bf16[4,128,512]{2,1,0:T(8,128)(2,1)} %bitcast.100), calls=%async_computation.2 | async-start | bytes 1048576 | tf_op jit(solution)/shard_map/all_to_all | solution.py:123
  100.8 4.3 %copy-start.9 = (bf16[4,128,512]{2,1,0:T(8,128)(2,1)}, bf16[4,128,512]{2,1,0:T(8,128)(2,1)S(1)}, u32[]{:S(2)}) copy-start(bf16[4,128,512]{2,1,0:T(8,128)(2,1)S(1)} %all-to-all-done.2) | copy-start | bytes 1572868
  100.8 20.0 %all-to-all-start.4 = ((bf16[4,128,512]{2,1,0:T(8,128)(2,1)}), bf16[4,128,512]{2,1,0:T(8,128)(2,1)}, u32[]{:S(2)}, u32[]{:S(2)}) async-start(bf16[4,128,512]{2,1,0:T(8,128)(2,1)} %bitcast.99), calls=%async_computation.4 | async-start | bytes 1048576 | tf_op jit(solution)/shard_map/all_to_all | solution.py:126
  116.0 2.1 %copy-start.8 = (bf16[512,4,128]{2,1,0:T(4,128)(2,1)S(1)}, bf16[512,4,128]{2,1,0:T(4,128)(2,1)}, u32[]{:S(2)}) copy-start(bf16[512,4,128]{2,1,0:T(4,128)(2,1)} %squeeze.14) | copy-start | bytes 1572868
  120.7 4.0 %copy-start.3 = (bf16[512,4,128]{2,1,0:T(4,128)(2,1)S(1)}, bf16[512,4,128]{2,1,0:T(4,128)(2,1)}, u32[]{:S(2)}) copy-start(bf16[512,4,128]{2,1,0:T(4,128)(2,1)} %copy-done.2) | copy-start | bytes 1572868
  124.7 3.5 %copy-start.4 = (f32[512,4,128]{2,0,1:T(8,128)S(1)}, f32[512,4,128]{2,0,1:T(8,128)}, u32[]{:S(2)}) copy-start(f32[512,4,128]{2,0,1:T(8,128)} %get-tuple-element.56) | copy-start | bytes 3145732
  128.2 7.2 %copy-start.10 = (bf16[512,4,128]{2,0,1:T(8,128)(2,1)S(1)}, bf16[512,4,128]{2,0,1:T(8,128)(2,1)}, u32[]{:S(2)}) copy-start(bf16[512,4,128]{2,0,1:T(8,128)(2,1)} %get-tuple-element.55) | copy-start | bytes 1572868
  130.5 18.4 %all-to-all-start.7 = ((bf16[4,128,512]{2,1,0:T(8,128)(2,1)}), bf16[4,128,512]{2,1,0:T(8,128)(2,1)S(1)}, u32[]{:S(2)}, u32[]{:S(2)}) async-start(bf16[4,128,512]{2,1,0:T(8,128)(2,1)} %reshape.425), calls=%async_computation.7 | async-start | bytes 1048576 | tf_op jit(solution)/shard_map/all_to_all | solution.py:155
  148.9 17.5 %all-to-all-start.3 = ((bf16[4,128,512]{2,1,0:T(8,128)(2,1)}), bf16[4,128,512]{2,1,0:T(8,128)(2,1)S(1)}, u32[]{:S(2)}, u32[]{:S(2)}) async-start(bf16[4,128,512]{2,1,0:T(8,128)(2,1)} %reshape.422), calls=%async_computation.3 | async-start | bytes 1048576 | tf_op jit(solution)/shard_map/all_to_all | solution.py:154
where the time goes:
time: 169 us; the launch traced here: 168 us
  waiting for transfers between devices  49.3 us (29%)
  blocking collectives  35.2 us (21%)
  local copies, waits for them, and re-layouts  31.4 us (19%)
  starting transfers between devices  25.9 us (15%)
  other arithmetic  12.5 us (7%)
  matrix products  11.7 us (7%)
    all_to_all x1, blocking collectives, body(): lax.all_to_all(qdot_send, 'seq', split_axis=0, concat_axis=1, tiled=True)  17.7 us
    all_to_all x1, blocking collectives, body(): lax.all_to_all(key_send, 'seq', split_axis=0, concat_axis=1, tiled=True)  17.5 us
    all_to_all x1, waiting for transfers between devices, body(): lax.all_to_all(to_sources(attended), 'seq', split_axis=0, concat_axis=0,...  12.7 us
    all_to_all x1, waiting for transfers between devices, body(): lax.all_to_all(to_sources(tangent_out), 'seq', split_axis=0, concat_axis=...  12.1 us
    all_to_all x1, waiting for transfers between devices, body(): lax.all_to_all(value_send, 'seq', split_axis=0, concat_axis=1, tiled=True)  10.2 us
    all_to_all x1, waiting for transfers between devices, body(): lax.all_to_all(kdot_send, 'seq', split_axis=0, concat_axis=1, tiled=True)  8.22 us
    all_to_all x1, starting transfers between devices, body(): lax.all_to_all(query_send, 'seq', split_axis=0, concat_axis=1, tiled=True)  6.35 us
    all_to_all x1, waiting for transfers between devices, body(): lax.all_to_all(query_send, 'seq', split_axis=0, concat_axis=1, tiled=True)  6.11 us
  transfers between devices with their start and end apart: 6, of which 5 were waited for; matrix products, arithmetic and copies ran while one was open for 20% of the time, Pallas kernels for 0%

commit v1 on v0

--- a/solution.py
+++ b/solution.py
@@ -119,7 +119,12 @@
 
     received = (
         lax.all_to_all(query_send, "seq", split_axis=0, concat_axis=1, tiled=True),
-        lax.all_to_all(key_send, "seq", split_axis=0, concat_axis=1, tiled=True),
+        jnp.concatenate(
+            lax.all_to_all(
+                jnp.stack(jnp.split(key_send, lax.axis_size("seq"), axis=0)), "seq", 0, 0
+            ),
+            axis=1,
+        ),
         lax.all_to_all(value_send, "seq", split_axis=0, concat_axis=1, tiled=True),
         lax.all_to_all(qdot_send, "seq", split_axis=0, concat_axis=1, tiled=True),
         lax.all_to_all(kdot_send, "seq", split_axis=0, concat_axis=1, tiled=True),

time: 169 us -> 162 us (0.959)
  blocking collectives: 35.2 us -> 0 us
  waiting for transfers between devices: 49.3 us -> 61.8 us
  starting transfers between devices: 25.9 us -> 33.6 us
  matrix products: 11.7 us -> 15.8 us
  other arithmetic: 12.5 us -> 16.2 us
    all_to_all x2 -> x0, blocking collectives: 35.2 us -> none  [the longest x1 17.7 us: body(): lax.all_to_all(qdot_send, 'seq', split_axis=0, concat_axis=1, tiled=True)]
    all_to_all x0 -> x2, waiting for transfers between devices: none -> 11.6 us  [the longest x1 7.19 us: body(): lax.all_to_all(jnp.stack(jnp.split(key_send, lax.axis_size('seq'), axis=0...]
    all_to_all x0 -> x2, starting transfers between devices: none -> 10.5 us  [the longest x1 6.35 us: body(): lax.all_to_all(jnp.stack(jnp.split(key_send, lax.axis_size('seq'), axis=0...]
    all_to_all x1, waiting for transfers between devices: 0.01 us -> 9.58 us  [body(): lax.all_to_all(vdot_send, 'seq', split_axis=0, concat_axis=1, tiled=True)]
    all_to_all x1, waiting for transfers between devices: 12.7 us -> 3.47 us  [body(): lax.all_to_all(to_sources(attended), 'seq', split_axis=0, concat_axis=0,...]
    all_to_all x1, waiting for transfers between devices: 8.22 us -> 0.01 us  [body(): lax.all_to_all(kdot_send, 'seq', split_axis=0, concat_axis=1, tiled=True)]
    all_to_all x1, waiting for transfers between devices: 6.11 us -> 11.7 us  [body(): lax.all_to_all(query_send, 'seq', split_axis=0, concat_axis=1, tiled=True)]
    sub x1, other arithmetic: 3.12 us -> 6.77 us  [primal_terms(): expons = jnp.exp(scores - largest)]
  transfers between devices with their start and end apart: 6 -> 8, of which waited for: 5 -> 7; matrix products, arithmetic and copies ran while one was open for 20% -> 32% of each run, Pallas kernels for 0% -> 0%
where the time goes in v1:
time: 162 us; the launch traced here: 161 us
  waiting for transfers between devices  61.8 us (38%)
  starting transfers between devices  33.6 us (21%)
  local copies, waits for them, and re-layouts  31.7 us (20%)
  other arithmetic  16.2 us (10%)
  matrix products  15.8 us (10%)
  between operations  1.67 us (1%)
    all_to_all x1, waiting for transfers between devices, body(): lax.all_to_all(value_send, 'seq', split_axis=0, concat_axis=1, tiled=True)  12.7 us
    all_to_all x1, waiting for transfers between devices, body(): lax.all_to_all(to_sources(tangent_out), 'seq', split_axis=0, concat_axis=...  12.7 us
    all_to_all x1, waiting for transfers between devices, body(): lax.all_to_all(query_send, 'seq', split_axis=0, concat_axis=1, tiled=True)  11.7 us
    all_to_all x1, waiting for transfers between devices, body(): lax.all_to_all(vdot_send, 'seq', split_axis=0, concat_axis=1, tiled=True)  9.58 us
    unnamed x24, local copies, waits for them, and re-layouts  7.34 us
    all_to_all x1, waiting for transfers between devices, body(): lax.all_to_all(jnp.stack(jnp.split(key_send, lax.axis_size('seq'), axis=0...  7.19 us
    sub x1, other arithmetic, primal_terms(): expons = jnp.exp(scores - largest)  6.77 us
    all_to_all x1, starting transfers between devices, body(): lax.all_to_all(jnp.stack(jnp.split(key_send, lax.axis_size('seq'), axis=0...  6.35 us
  transfers between devices with their start and end apart: 8, of which 7 were waited for; matrix products, arithmetic and copies ran while one was open for 32% of the time, Pallas kernels for 0%

profile of v1, /device:TPU:0, one launch (start us, length us, event | category | flops | bytes accessed | tf_op | source)
XLA Modules:
  0.0 160.8 jit_solution(4751909039980327634)
XLA Ops:
  1.4 1.3 copy.55
  2.8 0.2 fusion.45
  3.0 2.0 %copy.36 = bf16[1,128,2048]{1,2,0:T(8,128)(2,1)} copy(bf16[1,128,2048]{2,1,0:T(8,128)(2,1)} %param.8) | data formatting | bytes 1048576 | tf_op args[1]
  5.0 1.1 convert_element_type.162
  6.2 0.2 fusion.51
  6.4 0.2 maximum_negate_fusion.3
  6.6 0.3 maximum_negate_fusion.1
  6.9 0.3 fusion.40
  7.5 1.5 fusion.25
  9.0 0.9 pad_maximum_fusion.4
  9.9 6.3 %all-to-all-start.1 = ((bf16[4,1,128,512]{2,3,1,0:T(8,128)(2,1)}), bf16[4,1,128,512]{2,3,1,0:T(8,128)(2,1)}, u32[]{:S(2)}, u32[]{:S(2)}) async-start(bf16[4,1,128,512]{2,3,1,0:T(8,128)(2,1)} %pad_maximum_fusion.4), calls=%async_computation.1 | async-start | bytes 1048576 | tf_op jit(solution)/shard_map/all_to_all | solution.py:123
  16.2 0.2 copy.50
  16.4 1.5 fusion.48
  17.9 1.2 copy.33
  19.2 0.2 fusion.50
  19.4 1.0 copy-done.5
  20.4 0.3 copy-done.6
  20.7 0.3 maximum_negate_fusion.2
  21.0 0.3 maximum_negate_fusion
  21.3 0.6 copy-done.1
  21.9 1.7 %fusion.24 = (bf16[4,128,512]{1,2,0:T(8,128)(2,1)}, bf16[4,128,512]{1,2,0:T(8,128)(2,1)}) fusion(f32[1,128,4,512]{1,3,2,0:T(8,128)S(1)} %bitcast.131, f32[1,128,4,512]{1,3,2,0:T(8,128)S(1)} %bitcast.138, f32[1,128,4,512]{1,3,2,0:T(8,128)S(1)} %bitcast.139, f32[1,128,4,512]{1,3,2,0:T(8,128)S(1)} %bitcast.126, f32[1,128,4,512]{1,3,2,0:T(8,128)S(1)} %bitcast.133, ...), kind=kLoop, calls=%fused_computation.35 | loop fusion | flops 2621440 | bytes 9437696 | tf_op jit(solution)/shard_map/reshape | solution.py:97
  23.6 7.2 %all-to-all-done.1 = bf16[4,1,128,512]{2,3,1,0:T(8,128)(2,1)} async-done(((bf16[4,1,128,512]{2,3,1,0:T(8,128)(2,1)}), bf16[4,1,128,512]{2,3,1,0:T(8,128)(2,1)}, u32[]{:S(2)}, u32[]{:S(2)}) %all-to-all-start.1) | async-done | bytes 524320 | tf_op jit(solution)/shard_map/all_to_all | solution.py:123
  30.8 3.5 %all-to-all-start = ((bf16[4,128,512]{1,2,0:T(8,128)(2,1)}), bf16[4,128,512]{1,2,0:T(8,128)(2,1)S(1)}, u32[]{:S(2)}, u32[]{:S(2)}) async-start(bf16[4,128,512]{1,2,0:T(8,128)(2,1)} %get-tuple-element.25), calls=%async_computation | async-start | bytes 1048576 | tf_op jit(solution)/shard_map/all_to_all | solution.py:121
  34.3 1.4 reshape_squeeze.10
  35.7 0.9 copy.96
  36.6 11.7 %all-to-all-done = bf16[4,128,512]{1,2,0:T(8,128)(2,1)S(1)} async-done(((bf16[4,128,512]{1,2,0:T(8,128)(2,1)}), bf16[4,128,512]{1,2,0:T(8,128)(2,1)S(1)}, u32[]{:S(2)}, u32[]{:S(2)}) %all-to-all-start) | async-done | bytes 524320 | tf_op jit(solution)/shard_map/all_to_all | solution.py:121
  48.3 3.5 %all-to-all-start.2 = ((bf16[4,128,512]{2,1,0:T(8,128)(2,1)}), bf16[4,128,512]{2,1,0:T(8,128)(2,1)S(1)}, u32[]{:S(2)}, u32[]{:S(2)}) async-start(bf16[4,128,512]{2,1,0:T(8,128)(2,1)} %bitcast.112), calls=%async_computation.2 | async-start | bytes 1048576 | tf_op jit(solution)/shard_map/all_to_all | solution.py:128
  51.8 0.4 reshape_squeeze.23
  52.2 0.9 copy.95
  53.1 12.7 %all-to-all-done.2 = bf16[4,128,512]{2,1,0:T(8,128)(2,1)S(1)} async-done(((bf16[4,128,512]{2,1,0:T(8,128)(2,1)}), bf16[4,128,512]{2,1,0:T(8,128)(2,1)S(1)}, u32[]{:S(2)}, u32[]{:S(2)}) %all-to-all-start.2) | async-done | bytes 524320 | tf_op jit(solution)/shard_map/all_to_all | solution.py:128
  65.8 3.5 %all-to-all-start.4 = ((bf16[4,128,512]{2,1,0:T(8,128)(2,1)}), bf16[4,128,512]{2,1,0:T(8,128)(2,1)S(1)}, u32[]{:S(2)}, u32[]{:S(2)}) async-start(bf16[4,128,512]{2,1,0:T(8,128)(2,1)} %bitcast.111), calls=%async_computation.4 | async-start | bytes 1048576 | tf_op jit(solution)/shard_map/all_to_all | solution.py:131
  69.3 1.2 copy.39
  70.5 0.1 reshape_squeeze_reshape.3
  70.7 0.2 copy.35
  70.9 0.1 squeeze.13
  71.0 2.7 %fusion.35 = f32[4,512,512]{1,2,0:T(8,128)} fusion(bf16[512,4,128]{2,1,0:T(4,128)(2,1)S(1)} %reshape_squeeze_reshape.3, bf16[512,4,128]{2,1,0:T(4,128)(2,1)S(1)} %squeeze.13), kind=kOutput, calls=%fused_computation.49 | convolution fusion | flops 268435456 | bytes 5242880 | tf_op jit(solution)/shard_map/while/body/eval_jaxpr/bhd,khd->hbk/dot_general | solution.py:49
  73.7 9.6 %all-to-all-done.4 = bf16[4,128,512]{2,1,0:T(8,128)(2,1)S(1)} async-done(((bf16[4,128,512]{2,1,0:T(8,128)(2,1)}), bf16[4,128,512]{2,1,0:T(8,128)(2,1)S(1)}, u32[]{:S(2)}, u32[]{:S(2)}) %all-to-all-start.4) | async-done | bytes 524320 | tf_op jit(solution)/shard_map/all_to_all | solution.py:131
  83.3 4.1 %all-to-all-start.5 = ((bf16[4,128,512]{1,2,0:T(8,128)(2,1)}), bf16[4,128,512]{1,2,0:T(8,128)(2,1)}, u32[]{:S(2)}, u32[]{:S(2)}) async-start(bf16[4,128,512]{1,2,0:T(8,128)(2,1)} %get-tuple-element.24), calls=%async_computation.5 | async-start | bytes 1048576 | tf_op jit(solution)/shard_map/all_to_all | solution.py:129
  87.4 6.8 %fusion.53 = (f32[4,512]{1,0:T(4,128)S(1)}, f32[4,512,512]{1,2,0:T(8,128)}) fusion(f32[4,512,512]{1,2,0:T(8,128)} %fusion.35), kind=kOutput, calls=%fused_computation.87 | output fusion | flops 4194815 | bytes 8396800 | tf_op jit(solution)/shard_map/while/body/eval_jaxpr/sub | solution.py:53
  94.3 2.8 %divide_convert_fusion = bf16[4,512,512]{1,2,0:T(8,128)(2,1)S(1)} fusion(f32[4,512,512]{1,2,0:T(8,128)} %get-tuple-element.58, f32[4,512]{1,0:T(4,128)S(1)} %get-tuple-element.57), kind=kLoop, calls=%fused_computation.2 | loop fusion | flops 2097152 | bytes 6299648 | tf_op jit(solution)/shard_map/while/body/eval_jaxpr/convert_element_type | solution.py:55
  97.1 4.4 %all-to-all-done.5 = bf16[4,128,512]{1,2,0:T(8,128)(2,1)} async-done(((bf16[4,128,512]{1,2,0:T(8,128)(2,1)}), bf16[4,128,512]{1,2,0:T(8,128)(2,1)}, u32[]{:S(2)}, u32[]{:S(2)}) %all-to-all-start.5) | async-done | bytes 524320 | tf_op jit(solution)/shard_map/all_to_all | solution.py:129
  101.5 4.3 %all-to-all-start.6 = ((bf16[4,128,512]{1,2,0:T(8,128)(2,1)}), bf16[4,128,512]{1,2,0:T(8,128)(2,1)}, u32[]{:S(2)}, u32[]{:S(2)}) async-start(bf16[4,128,512]{1,2,0:T(8,128)(2,1)} %get-tuple-element.22), calls=%async_computation.6 | async-start | bytes 1048576 | tf_op jit(solution)/shard_map/all_to_all | solution.py:130
  105.9 1.9 %fusion.54 = (bf16[512,4,128]{2,0,1:T(8,128)(2,1)S(1)}, f32[512,4,128]{2,0,1:T(8,128)}) fusion(bf16[4,512,512]{1,2,0:T(8,128)(2,1)S(1)} %divide_convert_fusion, bf16[512,4,128]{2,1,0:T(4,128)(2,1)S(1)} %reshape_squeeze.22), kind=kOutput, calls=%fused_computation.88 | convolution fusion | flops 268697600 | bytes 4194304 | tf_op jit(solution)/shard_map/while/body/eval_jaxpr/hbk,khd->bhd/dot_general | solution.py:56
  107.8 1.2 copy.45
  109.0 2.0 %reshape.418 = bf16[4,128,512]{2,1,0:T(8,128)(2,1)} reshape(bf16[512,4,128]{2,1,0:T(4,128)(2,1)} %copy.45) | data formatting | bytes 1048576 | tf_op jit(solution)/shard_map/reshape | solution.py:156
  111.0 2.0 %copy.52 = bf16[4,128,512]{2,1,0:T(8,128)(2,1)} copy(bf16[4,128,512]{1,2,0:T(8,128)(2,1)} %all-to-all-done.5) | data formatting | bytes 1048576 | tf_op jit(solution)/shard_map/all_to_all | solution.py:129
  113.1 1.9 %squeeze.14 = bf16[512,4,128]{2,1,0:T(4,128)(2,1)} reshape(bf16[4,128,512]{2,1,0:T(8,128)(2,1)} %copy.52) | data formatting | bytes 1048576 | tf_op jit(solution)/shard_map/while/body/jit(dynamic_index_in_dim)/squeeze | solution.py:153
  115.0 2.0 %reshape_squeeze.24 = bf16[512,4,128]{2,1,0:T(4,128)(2,1)} reshape(bf16[4,128,512]{2,1,0:T(8,128)(2,1)} %copy-done.7) | data formatting | bytes 1048576 | tf_op jit(solution)/shard_map/reshape;squeeze | solution.py:115
  117.0 2.9 %fusion.30 = f32[4,512,128]{2,1,0:T(8,128)} fusion(bf16[4,512,512]{1,2,0:T(8,128)(2,1)S(1)} %divide_convert_fusion, bf16[512,4,128]{2,1,0:T(4,128)(2,1)} %reshape_squeeze.24), kind=kOutput, calls=%fused_computation.42 | convolution fusion | flops 268435456 | bytes 3670016 | tf_op jit(solution)/shard_map/while/body/eval_jaxpr/hbk,khd->bhd/dot_general | solution.py:71
  119.9 3.7 %fusion.28 = f32[4,512,512]{1,2,0:T(8,128)} fusion(bf16[512,4,128]{2,1,0:T(4,128)(2,1)} %squeeze.14, bf16[512,4,128]{2,1,0:T(4,128)(2,1)S(1)} %reshape_squeeze_reshape.3), kind=kOutput, calls=%fused_computation.40 | convolution fusion | flops 268435456 | bytes 5242880 | tf_op jit(solution)/shard_map/while/body/eval_jaxpr/bhd,khd->hbk/dot_general | solution.py:64
  123.7 4.9 %all-to-all-start.3 = ((bf16[4,128,512]{2,1,0:T(8,128)(2,1)}), bf16[4,128,512]{2,1,0:T(8,128)(2,1)S(1)}, u32[]{:S(2)}, u32[]{:S(2)}) async-start(bf16[4,128,512]{2,1,0:T(8,128)(2,1)} %reshape.418), calls=%async_computation.3 | async-start | bytes 1048576 | tf_op jit(solution)/shard_map/all_to_all | solution.py:159
  128.5 2.0 %copy.56 = bf16[4,128,512]{2,1,0:T(8,128)(2,1)} copy(bf16[4,128,512]{1,2,0:T(8,128)(2,1)} %all-to-all-done.6) | data formatting | bytes 1048576 | tf_op jit(solution)/shard_map/all_to_all | solution.py:130
  130.6 2.0 %reshape_squeeze.25 = bf16[512,4,128]{2,1,0:T(4,128)(2,1)} reshape(bf16[4,128,512]{2,1,0:T(8,128)(2,1)} %copy.56) | data formatting | bytes 1048576 | tf_op jit(solution)/shard_map/reshape;squeeze | solution.py:115
  132.5 3.7 %fusion.55 = (f32[4,512]{1,0:T(4,128)S(1)}, bf16[4,512,512]{1,2,0:T(8,128)(2,1)S(1)}) fusion(f32[4,512,512]{1,2,0:T(8,128)} %fusion.28, bf16[512,4,128]{2,1,0:T(4,128)(2,1)} %reshape_squeeze.25, bf16[512,4,128]{2,1,0:T(4,128)(2,1)} %copy-done.2, bf16[4,512,512]{1,2,0:T(8,128)(2,1)S(1)} %divide_convert_fusion), kind=kOutput, calls=%fused_computation.89 | convolution fusion | flops 274724864 | bytes 9445376 | tf_op jit(solution)/shard_map/while/body/eval_jaxpr/bhd,khd->hbk/dot_general | solution.py:65
  136.2 0.9 fusion.16
  137.1 0.4 copy.61
  137.5 1.0 reshape.421
  138.5 3.5 %all-to-all-done.3 = bf16[4,128,512]{2,1,0:T(8,128)(2,1)S(1)} async-done(((bf16[4,128,512]{2,1,0:T(8,128)(2,1)}), bf16[4,128,512]{2,1,0:T(8,128)(2,1)S(1)}, u32[]{:S(2)}, u32[]{:S(2)}) %all-to-all-start.3) | async-done | bytes 524320 | tf_op jit(solution)/shard_map/all_to_all | solution.py:159
  142.0 3.5 %all-to-all-start.7 = ((bf16[4,128,512]{2,1,0:T(8,128)(2,1)}), bf16[4,128,512]{2,1,0:T(8,128)(2,1)S(1)}, u32[]{:S(2)}, u32[]{:S(2)}) async-start(bf16[4,128,512]{2,1,0:T(8,128)(2,1)} %reshape.421), calls=%async_computation.7 | async-start | bytes 1048576 | tf_op jit(solution)/shard_map/all_to_all | solution.py:160
  145.5 0.3 copy.46
  145.8 1.0 copy.63
  146.8 12.7 %all-to-all-done.7 = bf16[4,128,512]{2,1,0:T(8,128)(2,1)S(1)} async-done(((bf16[4,128,512]{2,1,0:T(8,128)(2,1)}), bf16[4,128,512]{2,1,0:T(8,128)(2,1)S(1)}, u32[]{:S(2)}, u32[]{:S(2)}) %all-to-all-start.7) | async-done | bytes 524320 | tf_op jit(solution)/shard_map/all_to_all | solution.py:160
  159.5 0.3 copy.62
  159.8 1.0 copy.64
  (33 shorter events, 0.6 us)
Async XLA Ops:
  7.5 1.5 copy-start
  7.5 8.7 %copy-start.8 = (bf16[1,128,2048]{2,1,0:T(8,128)(2,1)S(1)}, bf16[1,128,2048]{2,1,0:T(8,128)(2,1)}, u32[]{:S(2)}) copy-start(bf16[1,128,2048]{2,1,0:T(8,128)(2,1)} %param.10) | copy-start | bytes 1572868
  9.9 20.9 %all-to-all-start.1 = ((bf16[4,1,128,512]{2,3,1,0:T(8,128)(2,1)}), bf16[4,1,128,512]{2,3,1,0:T(8,128)(2,1)}, u32[]{:S(2)}, u32[]{:S(2)}) async-start(bf16[4,1,128,512]{2,3,1,0:T(8,128)(2,1)} %pad_maximum_fusion.4), calls=%async_computation.1 | async-start | bytes 1048576 | tf_op jit(solution)/shard_map/all_to_all | solution.py:123
  19.2 1.2 copy-start.5
  19.2 1.5 copy-start.6
  20.7 1.2 copy-start.1
  23.6 28.2 %copy-start.9 = (bf16[1,128,2048]{2,1,0:T(8,128)(2,1)S(1)}, bf16[1,128,2048]{2,1,0:T(8,128)(2,1)}, u32[]{:S(2)}) copy-start(bf16[1,128,2048]{2,1,0:T(8,128)(2,1)} %param.12) | copy-start | bytes 1572868
  30.8 17.5 %all-to-all-start = ((bf16[4,128,512]{1,2,0:T(8,128)(2,1)}), bf16[4,128,512]{1,2,0:T(8,128)(2,1)S(1)}, u32[]{:S(2)}, u32[]{:S(2)}) async-start(bf16[4,128,512]{1,2,0:T(8,128)(2,1)} %get-tuple-element.25), calls=%async_computation | async-start | bytes 1048576 | tf_op jit(solution)/shard_map/all_to_all | solution.py:121
  48.3 17.5 %all-to-all-start.2 = ((bf16[4,128,512]{2,1,0:T(8,128)(2,1)}), bf16[4,128,512]{2,1,0:T(8,128)(2,1)S(1)}, u32[]{:S(2)}, u32[]{:S(2)}) async-start(bf16[4,128,512]{2,1,0:T(8,128)(2,1)} %bitcast.112), calls=%async_computation.2 | async-start | bytes 1048576 | tf_op jit(solution)/shard_map/all_to_all | solution.py:128
  65.8 17.5 %all-to-all-start.4 = ((bf16[4,128,512]{2,1,0:T(8,128)(2,1)}), bf16[4,128,512]{2,1,0:T(8,128)(2,1)S(1)}, u32[]{:S(2)}, u32[]{:S(2)}) async-start(bf16[4,128,512]{2,1,0:T(8,128)(2,1)} %bitcast.111), calls=%async_computation.4 | async-start | bytes 1048576 | tf_op jit(solution)/shard_map/all_to_all | solution.py:131
  71.0 16.4 %copy-start.2 = (bf16[512,4,128]{2,1,0:T(4,128)(2,1)}, bf16[512,4,128]{2,1,0:T(4,128)(2,1)S(1)}, u32[]{:S(2)}) copy-start(bf16[512,4,128]{2,1,0:T(4,128)(2,1)S(1)} %squeeze.13) | copy-start | bytes 1572868
  83.3 10.9 %copy-start.7 = (bf16[4,128,512]{2,1,0:T(8,128)(2,1)}, bf16[4,128,512]{2,1,0:T(8,128)(2,1)S(1)}, u32[]{:S(2)}) copy-start(bf16[4,128,512]{2,1,0:T(8,128)(2,1)S(1)} %all-to-all-done.4) | copy-start | bytes 1572868
  83.3 18.3 %all-to-all-start.5 = ((bf16[4,128,512]{1,2,0:T(8,128)(2,1)}), bf16[4,128,512]{1,2,0:T(8,128)(2,1)}, u32[]{:S(2)}, u32[]{:S(2)}) async-start(bf16[4,128,512]{1,2,0:T(8,128)(2,1)} %get-tuple-element.24), calls=%async_computation.5 | async-start | bytes 1048576 | tf_op jit(solution)/shard_map/all_to_all | solution.py:129
  101.5 22.1 %all-to-all-start.6 = ((bf16[4,128,512]{1,2,0:T(8,128)(2,1)}), bf16[4,128,512]{1,2,0:T(8,128)(2,1)}, u32[]{:S(2)}, u32[]{:S(2)}) async-start(bf16[4,128,512]{1,2,0:T(8,128)(2,1)} %get-tuple-element.22), calls=%async_computation.6 | async-start | bytes 1048576 | tf_op jit(solution)/shard_map/all_to_all | solution.py:130
  123.7 18.4 %all-to-all-start.3 = ((bf16[4,128,512]{2,1,0:T(8,128)(2,1)}), bf16[4,128,512]{2,1,0:T(8,128)(2,1)S(1)}, u32[]{:S(2)}, u32[]{:S(2)}) async-start(bf16[4,128,512]{2,1,0:T(8,128)(2,1)} %reshape.418), calls=%async_computation.3 | async-start | bytes 1048576 | tf_op jit(solution)/shard_map/all_to_all | solution.py:159
  132.5 3.7 %copy-start.3 = (f32[4,512,128]{2,1,0:T(8,128)S(1)}, f32[4,512,128]{2,1,0:T(8,128)}, u32[]{:S(2)}) copy-start(f32[4,512,128]{2,1,0:T(8,128)} %fusion.30) | copy-start | bytes 3145732
  132.5 3.7 %copy-start.4 = (f32[512,4,128]{2,0,1:T(8,128)S(1)}, f32[512,4,128]{2,0,1:T(8,128)}, u32[]{:S(2)}) copy-start(f32[512,4,128]{2,0,1:T(8,128)} %get-tuple-element.60) | copy-start | bytes 3145732
  142.0 17.5 %all-to-all-start.7 = ((bf16[4,128,512]{2,1,0:T(8,128)(2,1)}), bf16[4,128,512]{2,1,0:T(8,128)(2,1)S(1)}, u32[]{:S(2)}, u32[]{:S(2)}) async-start(bf16[4,128,512]{2,1,0:T(8,128)(2,1)} %reshape.421), calls=%async_computation.7 | async-start | bytes 1048576 | tf_op jit(solution)/shard_map/all_to_all | solution.py:160
